TPU v7x, 128 devices: a whole 4x4x4 slice. The times are simulated.
128 devices in a mesh: row: 16 (over y, x), col: 8 (over z, core).
Axes of the slice: x: 4, y: 4, z: 4, core: 2. Of those that a mesh axis runs over, the one named last changes fastest.
Arguments:
- row_emb: float32 [128, 300, 1024], P(('row', 'col')), may hold values from -1.5 to 1.5
- col_emb: float32 [128, 300, 1024], P(('row', 'col')), may hold values from -1.5 to 1.5
- row_acc: float32 [128, 300, 1024], P(('row', 'col')), may hold values from 0.5 to 8
- col_acc: float32 [128, 300, 1024], P(('row', 'col')), may hold values from 0.5 to 8
- marginal_log: float32 [131072], replicated, may hold values from -2 to 1
- tile_rows: int32 [384], P(('row', 'col')), may hold values from 0 to 127, as said below
- tile_cols: int32 [384], P(('row', 'col')), may hold values from 0 to 127, as said below
- counts: int32 [384, 1024, 1024], P(('row', 'col')), may hold values from 0 to 2047
Outputs:
- new_row_emb: float32 [128, 300, 1024], P(('row', 'col'))
- new_col_emb: float32 [128, 300, 1024], P(('row', 'col'))
- new_row_acc: float32 [128, 300, 1024], P(('row', 'col'))
- new_col_acc: float32 [128, 300, 1024], P(('row', 'col'))
Inputs may be any that keep to these rules, and one draw needn't show every extreme that they name: Block g of the embeddings lies on device g in the mesh's order (row slowest). Slot k lies on device p = k // 3; with p at row index r and col index c, tile_rows[k] // 8 equals r. With slot k on the device at col index c, tile_cols[k] % 8 equals c.
All inputs are finite; a program needn't handle non-finite values.
Results may differ from a plain program's by a relative error of at most 0.019.
Values may be sent and summed in bfloat16 or wider, within the bound.
No kernel may reach another device: no remote copies, remote signals or barrier semaphores. Data moves between devices by JAX's collectives and lax.ppermute only.
A program may use at most 128 MiB of HBM per device.

v0:
```python
import jax
import jax.numpy as jnp
from jax import lax
from jax.sharding import PartitionSpec as P

err_scale = 0.03125
learn_rate = 0.1


def split_up(array, dim, length):
    before, after = (array.shape[:dim], array.shape[dim + 1 :])
    return jnp.moveaxis(array.reshape(*before, length, -1, *after), dim, 0)


def sum_at_owner(array, axis, dim):
    length = lax.axis_size(axis)
    pieces = lax.all_to_all(split_up(array, dim, length), axis, 0, 0, tiled=True)
    return jnp.sum(pieces.astype(jnp.float32), axis=0)


def tile_terms(row_block, col_block, tile_counts, row_margin, col_margin):
    scores = lax.dot_general(
        row_block, col_block, (((0,), (0,)), ((), ())), preferred_element_type=jnp.float32
    )
    counted = tile_counts.astype(jnp.float32)
    shifted_log = jnp.log(jnp.maximum(counted, 1.0)) - row_margin[:, None] - col_margin[None, :]
    residue = scores - shifted_log
    weighted = (0.1 + 0.25 * jnp.sqrt(counted)) * residue
    cell_grad = jnp.where(tile_counts > 0, weighted, jax.nn.sigmoid(residue)) * err_scale
    errors = cell_grad.astype(jnp.bfloat16)
    row_term = lax.dot_general(
        col_block, errors, (((1,), (1,)), ((), ())), preferred_element_type=jnp.float32
    )
    col_term = jnp.dot(row_block, errors, preferred_element_type=jnp.float32)
    return (row_term, col_term)


def add_slot(buffer, slot_index, term):
    old_value = lax.dynamic_index_in_dim(buffer, slot_index, 0, keepdims=False)
    return lax.dynamic_update_index_in_dim(buffer, old_value + term, slot_index, 0)


def adagrad(weights, history, gradient):
    grown = history + gradient * gradient
    return (weights - learn_rate * gradient / jnp.sqrt(grown), grown)


def body(row_emb, col_emb, row_acc, col_acc, marginal_log, tile_rows, tile_cols, counts):
    col_count = lax.axis_size("col")
    row_count = lax.axis_size("row")
    emb_width = row_emb.shape[1]
    block_len = row_emb.shape[2]
    tile_total = counts.shape[0]
    row_low = row_emb.astype(jnp.bfloat16)
    col_low = col_emb.astype(jnp.bfloat16)
    rows_near = lax.all_gather(row_low, "col", axis=0, tiled=True)
    grads = (
        jnp.zeros((col_count, emb_width, block_len), jnp.float32),
        jnp.zeros((row_count, emb_width, block_len), jnp.float32),
    )
    cols_near = lax.all_gather(col_low, "row", axis=0, tiled=True)
    for tile_slot in range(tile_total):
        col_slot = tile_cols[tile_slot] // col_count
        col_block = lax.dynamic_index_in_dim(cols_near, col_slot, 0, keepdims=False)
        row_id = tile_rows[tile_slot]
        col_id = tile_cols[tile_slot]
        row_slot = row_id % col_count
        apply_col_slot = col_id // col_count
        row_block = lax.dynamic_index_in_dim(rows_near, row_slot, 0, keepdims=False)
        row_margin = lax.dynamic_slice_in_dim(marginal_log, row_id * block_len, block_len)
        col_margin = lax.dynamic_slice_in_dim(marginal_log, col_id * block_len, block_len)
        row_term, col_term = tile_terms(
            row_block, col_block, counts[tile_slot], row_margin, col_margin
        )
        grads = (
            add_slot(grads[0], row_slot, row_term),
            add_slot(grads[1], apply_col_slot, col_term),
        )
    row_sum = sum_at_owner(grads[0].astype(jnp.bfloat16), "col", 0)
    col_sum = lax.psum_scatter(
        grads[1].astype(jnp.bfloat16), "row", scatter_dimension=0, tiled=True
    ).astype(jnp.float32)
    new_row_emb, new_row_acc = adagrad(row_emb, row_acc, row_sum)
    new_col_emb, new_col_acc = adagrad(col_emb, col_acc, col_sum)
    return (new_row_emb, new_col_emb, new_row_acc, new_col_acc)


def solution(mesh):
    placed = (
        P(("row", "col"), None, None),
        P(("row", "col"), None, None),
        P(("row", "col"), None, None),
        P(("row", "col"), None, None),
        P(),
        P(("row", "col")),
        P(("row", "col")),
        P(("row", "col"), None, None),
    )
    return jax.shard_map(
        body,
        mesh=mesh,
        in_specs=placed,
        out_specs=(
            P(("row", "col"), None, None),
            P(("row", "col"), None, None),
            P(("row", "col"), None, None),
            P(("row", "col"), None, None),
        ),
        check_vma=False,
    )
```

profile of v0, /device:TPU:0, one launch (start us, length us, event | category | flops | bytes accessed | tf_op | source)
XLA Modules:
  0.0 274.2 jit_solution(9816080059861527763)
XLA Ops:
  7.2 2.3 copy.28
  9.6 2.3 copy.29
  12.0 0.6 fusion.64
  20.0 0.6 fusion.63
  30.0 0.8 fusion.62
  30.8 17.6 %all-gather.5.cloned.1.call-done = bf16[8,300,1024]{2,1,0:T(8,128)(2,1)} async-done(((bf16[1,300,1024]{2,1,0:T(8,128)(2,1)}), bf16[8,300,1024]{2,1,0:T(8,128)(2,1)}) %all-gather.5.cloned.1.call-update) | async-done | bytes 4915216 | tf_op jit(solution)/shard_map/all_gather | solution.py:56
  48.3 80.5 %all-gather.3.cloned.1.call-done = bf16[16,300,1024]{2,1,0:T(8,128)(2,1)} async-done(((bf16[1,300,1024]{2,1,0:T(8,128)(2,1)}), bf16[16,300,1024]{2,1,0:T(8,128)(2,1)}) %all-gather.3.cloned.1.call-update) | async-done | bytes 9830416 | tf_op jit(solution)/shard_map/all_gather | solution.py:61
  128.8 8.2 %fusion.14 = bf16[1024,1024]{1,0:T(8,128)(2,1)} fusion(s32[3,1024,1024]{2,1,0:T(8,128)} %param.15, f32[1024]{0:T(1024)S(1)} %get-tuple-element.17, f32[1024]{0:T(1024)S(1)} %get-tuple-element.18, bf16[8,300,1024]{2,1,0:T(8,128)(2,1)} %all-gather.5.cloned.1.call-done, s32[]{:T(128)S(6)} %select_n.95, ...), kind=kOutput, calls=%fused_computation.22 | convolution fusion | flops 644874240 | bytes 7544840 | tf_op jit(solution)/shard_map/dot_general | solution.py:22
  137.0 9.2 %broadcast_in_dim.36 = f32[16,300,1024]{2,1,0:T(8,128)} broadcast(f32[]{:T(128)} %constant.108.clone.1), dimensions={} | broadcast | bytes 19660804 | tf_op jit(solution)/shard_map/broadcast_in_dim | solution.py:59
  146.2 3.0 %fusion.23 = f32[16,300,1024]{2,1,0:T(8,128)} fusion(f32[16,300,1024]{2,1,0:T(8,128)} %broadcast_in_dim.36, s32[]{:T(128)S(6)} %select_n.93, bf16[1024,1024]{1,0:T(8,128)(2,1)S(1)} %copy-done.8, bf16[8,300,1024]{2,1,0:T(8,128)(2,1)} %all-gather.5.cloned.1.call-done, s32[]{:T(128)S(6)} %select_n.95), kind=kOutput, calls=%fused_computation.38 | convolution fusion | flops 629145600 | bytes 3964936 | tf_op jit(solution)/shard_map/dot_general | solution.py:34
  149.2 1.5 constant_dynamic-slice_fusion.3
  150.8 5.6 %fusion.9 = bf16[1024,1024]{1,0:T(8,128)(2,1)S(1)} fusion(s32[3,1024,1024]{2,1,0:T(8,128)S(1)} %bitcast.136, f32[1024]{0:T(1024)S(1)} %get-tuple-element.15, f32[1024]{0:T(1024)S(1)} %get-tuple-element.16, bf16[8,300,1024]{2,1,0:T(8,128)(2,1)} %all-gather.5.cloned.1.call-done, s32[]{:T(128)S(6)} %select_n.100, ...), kind=kOutput, calls=%fused_computation.15 | convolution fusion | flops 644874240 | bytes 7544840 | tf_op jit(solution)/shard_map/dot_general | solution.py:22
  156.4 0.5 slice-done.4
  156.9 1.9 fusion.18
  159.0 5.6 %fusion.4 = bf16[1024,1024]{1,0:T(8,128)(2,1)S(1)} fusion(s32[3,1024,1024]{2,1,0:T(8,128)S(1)} %bitcast.136, f32[1024]{0:T(1024)S(1)} %get-tuple-element.19, f32[1024]{0:T(1024)S(1)} %get-tuple-element.14, bf16[8,300,1024]{2,1,0:T(8,128)(2,1)} %all-gather.5.cloned.1.call-done, s32[]{:T(128)S(6)} %select_n.107, ...), kind=kOutput, calls=%fused_computation.8 | convolution fusion | flops 644874240 | bytes 7544840 | tf_op jit(solution)/shard_map/dot_general | solution.py:22
  164.6 1.3 copy-done.2
  165.9 1.9 fusion.16
  167.8 5.0 %convert_element_type.49 = bf16[16,300,1024]{2,1,0:T(8,128)(2,1)} convert(f32[16,300,1024]{2,1,0:T(8,128)S(1)} %fusion.16) | non-fusion elementwise | flops 4915200 | bytes 29491200 | tf_op jit(solution)/shard_map/convert_element_type | solution.py:81
  172.8 1.3 broadcast_in_dim.32
  174.4 1.9 fusion.24
  176.4 2.1 fusion.22
  178.6 1.9 fusion.20
  180.6 0.8 convert_bitcast_fusion
  181.4 62.3 %all_to_all.5 = bf16[8,1,300,1024]{3,2,1,0:T(8,128)(2,1)S(1)} all-to-all(bf16[8,1,300,1024]{3,2,1,0:T(8,128)(2,1)S(1)} %convert_bitcast_fusion), channel_id=1, replica_groups=mesh['row'=16,'col'=8] {'col'}, dimensions={0} | all-to-all | bytes 9830400 | tf_op jit(solution)/shard_map/all_to_all | solution.py:17
  243.7 1.1 convert_reduce_fusion
  244.9 0.4 multiply_bitcast_fusion
  245.2 0.5 copy-done.4
  245.8 5.8 %multiply_subtract_fusion = (f32[1,300,1024]{2,0,1:T(1,128)}, f32[1,300,1024]{2,0,1:T(1,128)}) fusion(f32[1,300,1024]{2,0,1:T(1,128)S(1)} %copy-done, f32[300,1024]{1,0:T(8,128)S(1)} %get-tuple-element.13, f32[1,300,1024]{2,0,1:T(1,128)S(1)} %copy-done.4, f32[1,300,1024]{2,1,0:T(8,128)S(1)} %get-tuple-element.12), kind=kLoop, calls=%fused_computation.47 | loop fusion | flops 921600 | bytes 7372800 | tf_op jit(solution)/shard_map/sub | solution.py:45
  251.6 9.8 %reduce-scatter.4.cloned.1.call-done = bf16[1,300,1024]{2,1,0:T(8,128)(2,1)} async-done(((bf16[16,300,1024]{2,1,0:T(8,128)(2,1)}), bf16[1,300,1024]{2,1,0:T(8,128)(2,1)}) %reduce-scatter.4.cloned.1.call-update) | async-done | bytes 614416
  261.4 1.8 fusion.26
  263.1 2.3 copy.21
  265.4 2.3 copy.22
  (44 shorter events, 0.9 us)
Async XLA Ops:
  7.2 4.8 %copy-start.6 = (s32[3]{0:T(128)S(1)}, s32[3]{0:T(128)}, u32[]{:S(2)}) copy-start(s32[3]{0:T(128)} %param.13) | copy-start | bytes 40
  7.2 12.9 %copy-start.7 = (s32[3]{0:T(128)S(1)}, s32[3]{0:T(128)}, u32[]{:S(2)}) copy-start(s32[3]{0:T(128)} %param.14) | copy-start | bytes 40
  7.2 41.2 %all-gather.5.cloned.1.call-start = ((), (), s32[]{:S(2)}) async-start(), calls=%async_computation.3 | async-start | bytes 5603328 | tf_op jit(solution)/shard_map/all_gather | solution.py:56
  9.6 119.3 %all-gather.3.cloned.1.call-start = ((), (), s32[]{:S(2)}) async-start(), calls=%async_computation.2 | async-start | bytes 10584064 | tf_op jit(solution)/shard_map/all_gather | solution.py:61
  11.9 249.4 %reduce-scatter.4.cloned.1.call-start = ((), (), s32[]{:S(2)}) async-start(), calls=%async_computation.4 | async-start | bytes 10584064
  128.8 21.9 %slice-start.5 = ((s8[12582912]{0:T(1024)(128)(4,1)}), s8[4194304]{0:T(1024)(128)(4,1)S(1)}, s32[]{:S(2)}) async-start(s8[12582912]{0:T(1024)(128)(4,1)} %bitcast.135), calls=%async_computation.10 | async-start | bytes 8388608
  128.8 21.9 %slice-start.6 = ((s8[12582912]{0:T(1024)(128)(4,1)}), s8[4194304]{0:T(1024)(128)(4,1)S(1)}, s32[]{:S(2)}) async-start(s8[12582912]{0:T(1024)(128)(4,1)} %bitcast.135), calls=%async_computation.11 | async-start | bytes 8388608
  137.0 9.3 %copy-start.8 = (bf16[1024,1024]{1,0:T(8,128)(2,1)S(1)}, bf16[1024,1024]{1,0:T(8,128)(2,1)}, u32[]{:S(2)}) copy-start(bf16[1024,1024]{1,0:T(8,128)(2,1)} %fusion.14) | copy-start | bytes 6291460
  137.0 13.8 %slice-start.7 = ((s8[12582912]{0:T(1024)(128)(4,1)}), s8[4194304]{0:T(1024)(128)(4,1)S(1)}, s32[]{:S(2)}) async-start(s8[12582912]{0:T(1024)(128)(4,1)} %bitcast.135), calls=%async_computation.12 | async-start | bytes 8388608
  149.2 7.2 %slice-start = ((s8[19922944]{0:T(1024)(128)(4,1)}), s8[4194304]{0:T(1024)(128)(4,1)S(1)}, s32[]{:S(2)}) async-start(s8[19922944]{0:T(1024)(128)(4,1)} %bitcast.133), calls=%async_computation.5 | async-start | bytes 8388608
  150.8 5.6 %slice-start.1 = ((s8[19922944]{0:T(1024)(128)(4,1)}), s8[4194304]{0:T(1024)(128)(4,1)S(1)}, s32[]{:S(2)}) async-start(s8[19922944]{0:T(1024)(128)(4,1)} %bitcast.133), calls=%async_computation.6 | async-start | bytes 8388608
  150.8 5.6 %slice-start.2 = ((s8[19922944]{0:T(1024)(128)(4,1)}), s8[4194304]{0:T(1024)(128)(4,1)S(1)}, s32[]{:S(2)}) async-start(s8[19922944]{0:T(1024)(128)(4,1)} %bitcast.133), calls=%async_computation.7 | async-start | bytes 8388608
  150.8 5.6 %slice-start.3 = ((s8[19922944]{0:T(1024)(128)(4,1)}), s8[4194304]{0:T(1024)(128)(4,1)S(1)}, s32[]{:S(2)}) async-start(s8[19922944]{0:T(1024)(128)(4,1)} %bitcast.133), calls=%async_computation.8 | async-start | bytes 8388608
  150.8 6.1 %slice-start.4 = ((s8[19922944]{0:T(1024)(128)(4,1)}), s8[3145728]{0:T(1024)(128)(4,1)S(1)}, s32[]{:S(2)}) async-start(s8[19922944]{0:T(1024)(128)(4,1)} %bitcast.133), calls=%async_computation.9 | async-start | bytes 6291456
  164.6 1.3 copy-start.2
  172.8 1.6 copy-start.9
  176.4 2.2 copy-start.3
  243.7 1.5 copy-start
  243.7 2.1 copy-start.4
  245.2 16.2 %copy-start.1 = (f32[1,300,1024]{2,0,1:T(1,128)S(1)}, f32[1,300,1024]{2,0,1:T(1,128)}, u32[]{:S(2)}) copy-start(f32[1,300,1024]{2,0,1:T(1,128)} %param.9) | copy-start | bytes 3686404
  245.2 16.1 %copy-start.5 = (f32[1,300,1024]{2,0,1:T(1,128)S(1)}, f32[1,300,1024]{2,0,1:T(1,128)}, u32[]{:S(2)}) copy-start(f32[1,300,1024]{2,0,1:T(1,128)} %param.11) | copy-start | bytes 3686404
Sparse Core Ops, SparseCore 0:
  10.3 38.0 all-gather.4
  51.0 77.7 all-gather.2
  172.9 88.4 reduce-scatter.3
where the time goes:
time: 275 us; the launch traced here: 274 us
  waiting for transfers between devices  108 us (39%)
  blocking collectives  62.3 us (23%)
  matrix products  32 us (12%)
  between operations  30.9 us (11%)
  local copies, waits for them, and re-layouts  26.2 us (10%)
  other arithmetic  14.8 us (5%)
    all_gather x1, waiting for transfers between devices, body(): cols_near = lax.all_gather(col_low, 'row', axis=0, tiled=True)  80.5 us
    all_to_all x1, blocking collectives, sum_at_owner(): lax.all_to_all(split_up(array, dim, length), axis, 0, 0, tiled=True)  62.3 us
    dot_general x3, matrix products, tile_terms(): lax.dot_general(row_block, col_block, (((0,), (0,)), ((), ())), preferred...  19.3 us
    all_gather x1, waiting for transfers between devices, body(): rows_near = lax.all_gather(row_low, 'col', axis=0, tiled=True)  17.6 us
    unnamed x40, local copies, waits for them, and re-layouts  11.9 us
    unnamed x4, waiting for transfers between devices  9.82 us
    broadcast_in_dim x1, local copies, waits for them, and re-layouts, body(): jnp.zeros((row_count, emb_width, block_len), jnp.float32)  9.25 us
    sub x2, other arithmetic, adagrad(): return (weights - learn_rate * gradient / jnp.sqrt(grown), grown)  7.58 us
  transfers between devices with their start and end apart: 3, of which 3 were waited for; matrix products, arithmetic and copies ran while one was open for 7% of the time, Pallas kernels for 0%

commit v1 on v0

--- a/solution.py
+++ b/solution.py
@@ -53,7 +53,11 @@
     tile_total = counts.shape[0]
     row_low = row_emb.astype(jnp.bfloat16)
     col_low = col_emb.astype(jnp.bfloat16)
-    rows_near = lax.all_gather(row_low, "col", axis=0, tiled=True)
+    count = lax.axis_size("col")
+    repeats = [count if d == 0 else 1 for d in range(row_low.ndim)]
+    rows_near = lax.all_to_all(
+        jnp.tile(row_low, repeats), "col", split_axis=0, concat_axis=0, tiled=True
+    )
     grads = (
         jnp.zeros((col_count, emb_width, block_len), jnp.float32),
         jnp.zeros((row_count, emb_width, block_len), jnp.float32),

time: 275 us -> 238 us (0.87)
  waiting for transfers between devices: 108 us -> 61.2 us
  starting transfers between devices: 0.12 us -> 5.63 us
    all_gather x1, waiting for transfers between devices: 80.5 us -> 12.6 us  [body(): cols_near = lax.all_gather(col_low, 'row', axis=0, tiled=True)]
    all_to_all x0 -> x1, waiting for transfers between devices: none -> 38.5 us  [body(): lax.all_to_all(jnp.tile(row_low, repeats), 'col', split_axis=0, concat_ax...]
    all_gather x1 -> x0, waiting for transfers between devices: 17.6 us -> none  [body(): rows_near = lax.all_gather(row_low, 'col', axis=0, tiled=True)]
    all_to_all x0 -> x1, starting transfers between devices: none -> 5.56 us  [body(): lax.all_to_all(jnp.tile(row_low, repeats), 'col', split_axis=0, concat_ax...]
    another operation x0 -> x1, local copies, waits for them, and re-layouts: none -> 2.89 us  [body(): jnp.tile(row_low, repeats)]
    unnamed x4 -> x3, waiting for transfers between devices: 9.82 us -> 10.2 us
  transfers between devices with their start and end apart: 3 -> 3, of which waited for: 3 -> 3; matrix products, arithmetic and copies ran while one was open for 7% -> 10% of each run, Pallas kernels for 0% -> 0%
where the time goes in v1:
time: 238 us; the launch traced here: 237 us
  blocking collectives  62.3 us (26%)
  waiting for transfers between devices  61.2 us (26%)
  matrix products  32 us (13%)
  between operations  32 us (13%)
  local copies, waits for them, and re-layouts  26.8 us (11%)
  other arithmetic  17 us (7%)
  starting transfers between devices  5.63 us (2%)
    all_to_all x1, blocking collectives, sum_at_owner(): lax.all_to_all(split_up(array, dim, length), axis, 0, 0, tiled=True)  62.3 us
    all_to_all x1, waiting for transfers between devices, body(): lax.all_to_all(jnp.tile(row_low, repeats), 'col', split_axis=0, concat_ax...  38.5 us
    dot_general x3, matrix products, tile_terms(): lax.dot_general(row_block, col_block, (((0,), (0,)), ((), ())), preferred...  19.3 us
    all_gather x1, waiting for transfers between devices, body(): cols_near = lax.all_gather(col_low, 'row', axis=0, tiled=True)  12.6 us
    unnamed x3, waiting for transfers between devices  10.2 us
    unnamed x40, local copies, waits for them, and re-layouts  9.65 us
    broadcast_in_dim x1, local copies, waits for them, and re-layouts, body(): jnp.zeros((row_count, emb_width, block_len), jnp.float32)  9.25 us
    sub x2, other arithmetic, adagrad(): return (weights - learn_rate * gradient / jnp.sqrt(grown), grown)  7.58 us
  transfers between devices with their start and end apart: 3, of which 3 were waited for; matrix products, arithmetic and copies ran while one was open for 10% of the time, Pallas kernels for 0%

profile of v1, /device:TPU:0, one launch (start us, length us, event | category | flops | bytes accessed | tf_op | source)
XLA Modules:
  0.0 237.1 jit_solution(12771290345418457833)
XLA Ops:
  7.2 2.3 copy.28
  9.5 2.1 convert_element_type.41
  11.9 2.9 %tile.10 = bf16[8,300,1024]{2,1,0:T(8,128)(2,1)} broadcast(bf16[300,1024]{1,0:T(8,128)(2,1)S(1)} %bitcast.138), dimensions={1,2} | broadcast | bytes 5529600 | tf_op jit(solution)/shard_map/tile | solution.py:59
  14.8 5.6 %all-to-all-start = ((bf16[8,300,1024]{2,1,0:T(8,128)(2,1)}), bf16[8,300,1024]{2,1,0:T(8,128)(2,1)}, u32[]{:S(2)}, u32[]{:S(2)}) async-start(bf16[8,300,1024]{2,1,0:T(8,128)(2,1)} %tile.10), calls=%async_computation | async-start | bytes 9961472 | tf_op jit(solution)/shard_map/all_to_all | solution.py:58
  20.4 0.6 fusion.64
  28.8 0.6 fusion.63
  39.2 0.8 fusion.62
  40.0 38.5 %all-to-all-done = bf16[8,300,1024]{2,1,0:T(8,128)(2,1)} async-done(((bf16[8,300,1024]{2,1,0:T(8,128)(2,1)}), bf16[8,300,1024]{2,1,0:T(8,128)(2,1)}, u32[]{:S(2)}, u32[]{:S(2)}) %all-to-all-start) | async-done | bytes 4915232 | tf_op jit(solution)/shard_map/all_to_all | solution.py:58
  78.5 12.6 %all-gather.2.cloned.1.call-done = bf16[16,300,1024]{2,1,0:T(8,128)(2,1)} async-done(((bf16[1,300,1024]{2,1,0:T(8,128)(2,1)}), bf16[16,300,1024]{2,1,0:T(8,128)(2,1)}) %all-gather.2.cloned.1.call-update) | async-done | bytes 9830416 | tf_op jit(solution)/shard_map/all_gather | solution.py:65
  91.1 8.2 %fusion.14 = bf16[1024,1024]{1,0:T(8,128)(2,1)} fusion(s32[3,1024,1024]{2,1,0:T(8,128)} %param.15, f32[1024]{0:T(1024)S(1)} %get-tuple-element.17, f32[1024]{0:T(1024)S(1)} %get-tuple-element.18, bf16[8,300,1024]{2,1,0:T(8,128)(2,1)} %all-to-all-done, s32[]{:T(128)S(6)} %select_n.95, bf16[16,300,1024]{2,1,0:T(8,128)(2,1)} %all-gather.2.cloned.1.call-done, ...), kind=kOutput, calls=%fused_computation.22 | convolution fusion | flops 644874240 | bytes 7544840 | tf_op jit(solution)/shard_map/dot_general | solution.py:22
  99.2 9.3 %broadcast_in_dim.36 = f32[16,300,1024]{2,1,0:T(8,128)} broadcast(f32[]{:T(128)} %constant.108.clone.1), dimensions={} | broadcast | bytes 19660804 | tf_op jit(solution)/shard_map/broadcast_in_dim | solution.py:63
  108.5 3.0 %fusion.23 = f32[16,300,1024]{2,1,0:T(8,128)} fusion(f32[16,300,1024]{2,1,0:T(8,128)} %broadcast_in_dim.36, s32[]{:T(128)S(6)} %select_n.93, bf16[1024,1024]{1,0:T(8,128)(2,1)S(1)} %copy-done.8, bf16[8,300,1024]{2,1,0:T(8,128)(2,1)} %all-to-all-done, s32[]{:T(128)S(6)} %select_n.95), kind=kOutput, calls=%fused_computation.38 | convolution fusion | flops 629145600 | bytes 3964936 | tf_op jit(solution)/shard_map/dot_general | solution.py:34
  111.5 1.5 constant_dynamic-slice_fusion.3
  113.1 5.6 %fusion.9 = bf16[1024,1024]{1,0:T(8,128)(2,1)S(1)} fusion(s32[3,1024,1024]{2,1,0:T(8,128)S(1)} %bitcast.140, f32[1024]{0:T(1024)S(1)} %get-tuple-element.15, f32[1024]{0:T(1024)S(1)} %get-tuple-element.16, bf16[8,300,1024]{2,1,0:T(8,128)(2,1)} %all-to-all-done, s32[]{:T(128)S(6)} %select_n.100, bf16[16,300,1024]{2,1,0:T(8,128)(2,1)} %all-gather.2.cloned.1.call-done, ...), kind=kOutput, calls=%fused_computation.15 | convolution fusion | flops 644874240 | bytes 7544840 | tf_op jit(solution)/shard_map/dot_general | solution.py:22
  118.7 0.5 slice-done.4
  119.2 1.9 fusion.18
  121.2 5.6 %fusion.4 = bf16[1024,1024]{1,0:T(8,128)(2,1)S(1)} fusion(s32[3,1024,1024]{2,1,0:T(8,128)S(1)} %bitcast.140, f32[1024]{0:T(1024)S(1)} %get-tuple-element.19, f32[1024]{0:T(1024)S(1)} %get-tuple-element.14, bf16[8,300,1024]{2,1,0:T(8,128)(2,1)} %all-to-all-done, s32[]{:T(128)S(6)} %select_n.107, bf16[16,300,1024]{2,1,0:T(8,128)(2,1)} %all-gather.2.cloned.1.call-done, ...), kind=kOutput, calls=%fused_computation.8 | convolution fusion | flops 644874240 | bytes 7544840 | tf_op jit(solution)/shard_map/dot_general | solution.py:22
  126.8 1.3 copy-done.2
  128.1 1.9 fusion.16
  130.0 5.0 %convert_element_type.49 = bf16[16,300,1024]{2,1,0:T(8,128)(2,1)} convert(f32[16,300,1024]{2,1,0:T(8,128)S(1)} %fusion.16) | non-fusion elementwise | flops 4915200 | bytes 29491200 | tf_op jit(solution)/shard_map/convert_element_type | solution.py:85
  135.1 1.3 broadcast_in_dim.32
  136.7 1.9 fusion.24
  138.7 2.1 fusion.22
  140.9 1.9 fusion.20
  142.9 0.8 convert_bitcast_fusion
  143.6 62.3 %all_to_all.10 = bf16[8,1,300,1024]{3,2,1,0:T(8,128)(2,1)S(1)} all-to-all(bf16[8,1,300,1024]{3,2,1,0:T(8,128)(2,1)S(1)} %convert_bitcast_fusion), channel_id=1, replica_groups=mesh['row'=16,'col'=8] {'col'}, dimensions={0} | all-to-all | bytes 9830400 | tf_op jit(solution)/shard_map/all_to_all | solution.py:17
  206.0 1.1 convert_reduce_fusion
  207.9 5.8 %multiply_subtract_fusion = (f32[1,300,1024]{2,0,1:T(1,128)}, f32[1,300,1024]{2,0,1:T(1,128)}) fusion(f32[1,300,1024]{2,0,1:T(1,128)S(1)} %copy-done, f32[300,1024]{1,0:T(8,128)S(1)} %get-tuple-element.13, f32[1,300,1024]{2,0,1:T(1,128)S(1)} %copy-done.4, f32[1,300,1024]{2,1,0:T(8,128)S(1)} %get-tuple-element.12), kind=kLoop, calls=%fused_computation.46 | loop fusion | flops 921600 | bytes 7372800 | tf_op jit(solution)/shard_map/sub | solution.py:45
  213.7 10.1 %reduce-scatter.4.cloned.1.call-done = bf16[1,300,1024]{2,1,0:T(8,128)(2,1)} async-done(((bf16[16,300,1024]{2,1,0:T(8,128)(2,1)}), bf16[1,300,1024]{2,1,0:T(8,128)(2,1)}) %reduce-scatter.4.cloned.1.call-update) | async-done | bytes 614416
  223.9 1.8 fusion.26
  225.6 2.3 copy.20
  227.9 2.3 copy.21
  (45 shorter events, 1.8 us)
Async XLA Ops:
  7.2 83.9 %all-gather.2.cloned.1.call-start = ((), (), s32[]{:S(2)}) async-start(), calls=%async_computation.3 | async-start | bytes 10584064 | tf_op jit(solution)/shard_map/all_gather | solution.py:65
  14.8 5.6 %copy-start.6 = (s32[3]{0:T(128)S(1)}, s32[3]{0:T(128)}, u32[]{:S(2)}) copy-start(s32[3]{0:T(128)} %param.13) | copy-start | bytes 40
  14.8 14.0 %copy-start.7 = (s32[3]{0:T(128)S(1)}, s32[3]{0:T(128)}, u32[]{:S(2)}) copy-start(s32[3]{0:T(128)} %param.14) | copy-start | bytes 40
  14.8 63.7 %all-to-all-start = ((bf16[8,300,1024]{2,1,0:T(8,128)(2,1)}), bf16[8,300,1024]{2,1,0:T(8,128)(2,1)}, u32[]{:S(2)}, u32[]{:S(2)}) async-start(bf16[8,300,1024]{2,1,0:T(8,128)(2,1)} %tile.10), calls=%async_computation | async-start | bytes 9961472 | tf_op jit(solution)/shard_map/all_to_all | solution.py:58
  20.3 203.5 %reduce-scatter.4.cloned.1.call-start = ((), (), s32[]{:S(2)}) async-start(), calls=%async_computation.4 | async-start | bytes 10584064
  91.1 21.9 %slice-start.5 = ((s8[12582912]{0:T(1024)(128)(4,1)}), s8[4194304]{0:T(1024)(128)(4,1)S(1)}, s32[]{:S(2)}) async-start(s8[12582912]{0:T(1024)(128)(4,1)} %bitcast.139), calls=%async_computation.10 | async-start | bytes 8388608
  91.1 21.9 %slice-start.6 = ((s8[12582912]{0:T(1024)(128)(4,1)}), s8[4194304]{0:T(1024)(128)(4,1)S(1)}, s32[]{:S(2)}) async-start(s8[12582912]{0:T(1024)(128)(4,1)} %bitcast.139), calls=%async_computation.11 | async-start | bytes 8388608
  99.2 9.3 %copy-start.8 = (bf16[1024,1024]{1,0:T(8,128)(2,1)S(1)}, bf16[1024,1024]{1,0:T(8,128)(2,1)}, u32[]{:S(2)}) copy-start(bf16[1024,1024]{1,0:T(8,128)(2,1)} %fusion.14) | copy-start | bytes 6291460
  99.2 13.8 %slice-start.7 = ((s8[12582912]{0:T(1024)(128)(4,1)}), s8[4194304]{0:T(1024)(128)(4,1)S(1)}, s32[]{:S(2)}) async-start(s8[12582912]{0:T(1024)(128)(4,1)} %bitcast.139), calls=%async_computation.12 | async-start | bytes 8388608
  111.5 7.2 %slice-start = ((s8[19922944]{0:T(1024)(128)(4,1)}), s8[4194304]{0:T(1024)(128)(4,1)S(1)}, s32[]{:S(2)}) async-start(s8[19922944]{0:T(1024)(128)(4,1)} %bitcast.136), calls=%async_computation.5 | async-start | bytes 8388608
  113.0 5.6 %slice-start.1 = ((s8[19922944]{0:T(1024)(128)(4,1)}), s8[4194304]{0:T(1024)(128)(4,1)S(1)}, s32[]{:S(2)}) async-start(s8[19922944]{0:T(1024)(128)(4,1)} %bitcast.136), calls=%async_computation.6 | async-start | bytes 8388608
  113.0 5.6 %slice-start.2 = ((s8[19922944]{0:T(1024)(128)(4,1)}), s8[4194304]{0:T(1024)(128)(4,1)S(1)}, s32[]{:S(2)}) async-start(s8[19922944]{0:T(1024)(128)(4,1)} %bitcast.136), calls=%async_computation.7 | async-start | bytes 8388608
  113.0 5.6 %slice-start.3 = ((s8[19922944]{0:T(1024)(128)(4,1)}), s8[4194304]{0:T(1024)(128)(4,1)S(1)}, s32[]{:S(2)}) async-start(s8[19922944]{0:T(1024)(128)(4,1)} %bitcast.136), calls=%async_computation.8 | async-start | bytes 8388608
  113.1 6.1 %slice-start.4 = ((s8[19922944]{0:T(1024)(128)(4,1)}), s8[3145728]{0:T(1024)(128)(4,1)S(1)}, s32[]{:S(2)}) async-start(s8[19922944]{0:T(1024)(128)(4,1)} %bitcast.136), calls=%async_computation.9 | async-start | bytes 6291456
  126.8 1.3 copy-start.2
  135.1 1.6 copy-start.9
  138.7 2.2 copy-start.3
  206.0 1.5 copy-start
  206.0 1.9 copy-start.4
  207.5 16.4 %copy-start.1 = (f32[1,300,1024]{2,0,1:T(1,128)S(1)}, f32[1,300,1024]{2,0,1:T(1,128)}, u32[]{:S(2)}) copy-start(f32[1,300,1024]{2,0,1:T(1,128)} %param.9) | copy-start | bytes 3686404
  207.5 16.4 %copy-start.5 = (f32[1,300,1024]{2,0,1:T(1,128)S(1)}, f32[1,300,1024]{2,0,1:T(1,128)}, u32[]{:S(2)}) copy-start(f32[1,300,1024]{2,0,1:T(1,128)} %param.11) | copy-start | bytes 3686404
Sparse Core Ops, SparseCore 0:
  10.7 80.3 all-gather.1
  135.2 88.6 reduce-scatter.3
